TPU v7x, 32 devices: a whole 2x2x4 slice. The times are simulated.
32 devices in a mesh: grow: 4 (over z), gy: 4 (over x, core), gz: 2 (over y).
Axes of the slice: x: 2, y: 2, z: 4, core: 2. Of those that a mesh axis runs over, the one named last changes fastest.
Arguments:
- labels: int32 [128, 32, 256], P('grow', 'gy', 'gz'), may hold values from 0 to 3
- potential: float32 [2, 128, 32, 256], P(None, 'grow', 'gy', 'gz'), may hold values from -3 to 3
- melt_codes: int32 [16, 32, 256], P(None, 'gy', 'gz'), may hold values from 0 to 7
- melt_table: float32 [2, 8], replicated, may hold values from -1 to 1
Outputs:
- phases: float32 [4, 128, 32, 256], P(None, 'grow', 'gy', 'gz')
- potentials: float32 [2, 128, 32, 256], P(None, 'grow', 'gy', 'gz')
All inputs are finite; a program needn't handle non-finite values.
Results may differ from a plain program's by a relative error of at most 0.0001.
Values sent between devices are 32-bit elements; how exact they have to be, the bound alone decides.
A program may use at most 64 MiB of HBM per device.

v0:
```python
import jax
import jax.numpy as jnp
from jax import lax
from jax.sharding import PartitionSpec as P

SHIFT = 16
STEPS_BEFORE = 3


comp_table = ((0.8, 0.1), (0.1, 0.8), (0.1, 0.1), (0.35, 0.35))
free_energy = (-0.05, -0.05, -0.05, 0.0)
diffusivity = (0.05, 0.05, 0.05, 1.0)
grad_rate = 0.12
well_rate = 0.3
drive_rate = 0.5
diff_rate = 0.15


def with_halo(block, sides, width, periodic):
    for axis, dim in sides:
        count = lax.axis_size(axis)
        forward = [(i, i + 1) for i in range(count - 1)]
        if periodic:
            forward.append((count - 1, 0))
        backward = [(target, source) for source, target in forward]
        low = lax.ppermute(
            lax.slice_in_dim(block, block.shape[dim] - width, None, axis=dim), axis, forward
        )
        high = lax.ppermute(lax.slice_in_dim(block, 0, width, axis=dim), axis, backward)
        block = jnp.concatenate([low, block, high], axis=dim)
    return block


def shifted_2(value, axis, steps):
    count = lax.axis_size(axis)
    first, last = (max(0, -steps), min(count, count - steps))
    return lax.ppermute(value, axis, [(source, source + steps) for source in range(first, last)])


def laplacian(fields, grow_padded, side_padded):
    total = grow_padded[:, 2:] + grow_padded[:, :-2]
    total = total + (side_padded[:, :, 2:, 1:-1] + side_padded[:, :, :-2, 1:-1])
    total = total + (side_padded[:, :, 1:-1, 2:] + side_padded[:, :, 1:-1, :-2])
    return total - 6.0 * fields


def advance(fields, grow_padded, side_padded):
    phases = fields[:4]
    chem_pot = fields[4:]
    laplace = laplacian(fields, grow_padded, side_padded)
    comp = jnp.array(comp_table, jnp.float32)
    comp_first = comp[:, 0].reshape(4, 1, 1, 1)
    comp_second = comp[:, 1].reshape(4, 1, 1, 1)
    energy = jnp.array(free_energy, jnp.float32).reshape(4, 1, 1, 1)
    spread = jnp.array(diffusivity, jnp.float32).reshape(4, 1, 1, 1)
    grand_pot = energy - (chem_pot[0:1] * comp_first + chem_pot[1:2] * comp_second)
    squares = phases * phases
    others = jnp.sum(squares, axis=0, keepdims=True) - squares
    slope = 6.0 * phases * (1.0 - phases)
    increment = (
        grad_rate * laplace[:4] - 2.0 * well_rate * phases * others - drive_rate * slope * grand_pot
    )
    increment = increment - jnp.mean(increment, axis=0, keepdims=True)
    clipped = jnp.clip(phases + increment, 0.0, 1.0)
    new_phases = clipped / jnp.sum(clipped, axis=0, keepdims=True)
    change = new_phases * new_phases * (3.0 - 2.0 * new_phases) - phases * phases * (
        3.0 - 2.0 * phases
    )
    mobility = jnp.sum(phases * spread, axis=0, keepdims=True)
    release = jnp.concatenate(
        [
            jnp.sum(change * comp_first, axis=0, keepdims=True),
            jnp.sum(change * comp_second, axis=0, keepdims=True),
        ],
        axis=0,
    )
    new_chem = chem_pot + diff_rate * mobility * laplace[4:] - release
    return jnp.concatenate([new_phases, new_chem], axis=0)


def melt_planes(melt_codes, melt_table):
    levels = melt_table.shape[1]
    onehot = (
        melt_codes[None] == jnp.arange(levels, dtype=jnp.int32).reshape(levels, 1, 1, 1)
    ).astype(jnp.float32)
    chem_pot = jnp.einsum("ik,kabc->iabc", melt_table, onehot, precision=lax.Precision.HIGHEST)
    liquid = (jnp.arange(4, dtype=jnp.int32) == 3).astype(jnp.float32).reshape(4, 1, 1, 1)
    phases = jnp.broadcast_to(liquid, (4,) + melt_codes.shape)
    return jnp.concatenate([phases, chem_pot], axis=0)


def side_faces(fields):
    return with_halo(fields, (("gy", 2), ("gz", 3)), 1, True)


def on_device(labels, potential, melt_codes, melt_table):
    index_grow = lax.axis_index("grow")
    is_first = index_grow == 0
    is_last = index_grow == lax.axis_size("grow") - 1

    def faces(fields):
        raw_grow = with_halo(fields, (("grow", 1),), 1, False)
        side_padded = side_faces(fields)
        low_ghost = jnp.where(is_first, fields[:, :1], raw_grow[:, :1])
        top_ghost = jnp.where(is_last, fields[:, -1:], raw_grow[:, -1:])
        return (jnp.concatenate([low_ghost, fields, top_ghost], axis=1), side_padded)

    phases = (labels[None] == jnp.arange(4, dtype=jnp.int32).reshape(4, 1, 1, 1)).astype(
        jnp.float32
    )
    fields = jnp.concatenate([phases, potential], axis=0)
    for iteration in range(STEPS_BEFORE):
        grow_padded, side_padded = faces(fields)
        fields = advance(fields, grow_padded, side_padded)
    melt_block = melt_planes(melt_codes, melt_table)
    arrived = shifted_2(fields[:, : SHIFT + 1], "grow", -1)
    incoming = jnp.where(is_last, melt_block, arrived[:, :SHIFT])
    shifted = jnp.concatenate([fields[:, SHIFT:], incoming], axis=1)
    low_ghost = jnp.where(is_first, shifted[:, :1], fields[:, SHIFT - 1 : SHIFT])
    top_ghost = jnp.where(is_last, incoming[:, -1:], arrived[:, SHIFT : SHIFT + 1])
    grow_padded = jnp.concatenate([low_ghost, shifted, top_ghost], axis=1)
    fields = advance(shifted, grow_padded, side_faces(shifted))
    grow_padded, side_padded = faces(fields)
    fields = advance(fields, grow_padded, side_padded)
    return (fields[:4], fields[4:])


def solution(mesh):
    return jax.shard_map(
        on_device,
        mesh=mesh,
        in_specs=(P("grow", "gy", "gz"), P(None, "grow", "gy", "gz"), P(None, "gy", "gz"), P()),
        out_specs=(P(None, "grow", "gy", "gz"), P(None, "grow", "gy", "gz")),
        check_vma=False,
    )
```

profile of v0, /device:TPU:0, one launch (start us, length us, event | category | flops | bytes accessed | tf_op | source)
XLA Modules:
  0.0 115.4 jit_solution(27232296005817605)
XLA Ops:
  4.0 2.5 %collective-permute-start.2 = (f32[6,32,1,128]{3,1,2,0:T(8,128)S(1)}, f32[6,32,1,128]{3,1,2,0:T(8,128)}, u32[]{:S(2)}, u32[]{:S(2)}) collective-permute-start(f32[6,32,1,128]{3,1,2,0:T(8,128)S(1)} %get-tuple-element.70), channel_id=1, source_target_pairs={{2,0},{4,2},{6,4},{0,6},{3,1},{5,3},{7,5},{1,7},{10,8},{12,10},{14... | collective-permute-start | bytes 294920 | tf_op jit(solution)/shard_map/ppermute | solution.py:29
  6.6 2.8 %collective-permute-done = f32[6,1,8,128]{3,1,2,0:T(1,128)S(1)} collective-permute-done((f32[6,1,8,128]{3,1,2,0:T(1,128)S(1)}, f32[6,1,8,128]{3,1,2,0:T(1,128)S(1)}, u32[]{:S(2)}, u32[]{:S(2)}) %collective-permute-start) | collective-permute-done | bytes 24608 | tf_op jit(solution)/shard_map/ppermute | solution.py:29
  10.1 4.5 %collective-permute-start.1 = (f32[6,1,8,128]{3,1,2,0:T(1,128)}, f32[6,1,8,128]{3,1,2,0:T(1,128)}, u32[]{:S(2)}, u32[]{:S(2)}) collective-permute-start(f32[6,1,8,128]{3,1,2,0:T(1,128)} %get-tuple-element.48), channel_id=1, source_target_pairs={{0,8},{8,16},{16,24},{1,9},{9,17},{17,25},{2,10},{10,18},{18,26},{... | collective-permute-start | bytes 73736 | tf_op jit(solution)/shard_map/ppermute | solution.py:26
  17.1 1.5 %collective-permute-start.4 = (f32[6,32,10,1]{1,0,3,2:T(8,128)}, f32[6,32,10,1]{1,0,3,2:T(8,128)S(1)}, u32[]{:S(2)}, u32[]{:S(2)}) collective-permute-start(f32[6,32,10,1]{1,0,3,2:T(8,128)} %copy.52), channel_id=1, source_target_pairs={{1,0},{0,1},{3,2},{2,3},{5,4},{4,5},{7,6},{6,7},{9,8},{8,9},{11,10... | collective-permute-start | bytes 23048 | tf_op jit(solution)/shard_map/ppermute | solution.py:29
  21.8 1.6 %collective-permute-done.5 = f32[6,32,10,1]{1,0,3,2:T(8,128)} collective-permute-done((f32[6,32,10,1]{1,0,3,2:T(8,128)S(1)}, f32[6,32,10,1]{1,0,3,2:T(8,128)}, u32[]{:S(2)}, u32[]{:S(2)}) %collective-permute-start.5) | collective-permute-done | bytes 7712 | tf_op jit(solution)/shard_map/ppermute | solution.py:26
  24.6 1.7 %fusion.7 = f32[6,32,8,128]{3,1,2,0:T(8,128)S(1)} fusion(f32[2,32,8,128]{3,1,2,0:T(8,128)S(1)} %copy.51, f32[4,32,8,128]{3,1,2,0:T(8,128)S(1)} %fusion.56, f32[6,32,10,1]{3,1,2,0:T(8,128)S(1)} %copy.55, f32[6,32,1,128]{3,1,2,0:T(8,128)} %collective-permute-done.2, f32[6,32,1,128]{3,1,2,0:T(8,128)} %collective-permute-done.3, f32[6,32,10,1]{3,1,2,0:T(8,128)S(1)} %copy.53, ...), kind=kLoop, calls=%fused_computation.68 | loop fusion | flops 4718592 | bytes 1833984 | tf_op jit(solution)/shard_map/sub | solution.py:44
  29.8 3.8 %collective-permute-done.6 = f32[6,1,8,128]{3,1,2,0:T(1,128)S(1)} collective-permute-done((f32[6,1,8,128]{3,1,2,0:T(1,128)S(1)}, f32[6,1,8,128]{3,1,2,0:T(1,128)S(1)}, u32[]{:S(2)}, u32[]{:S(2)}) %collective-permute-start.6) | collective-permute-done | bytes 24608 | tf_op jit(solution)/shard_map/ppermute | solution.py:29
  33.7 2.9 %collective-permute-start.7 = (f32[6,1,8,128]{3,1,2,0:T(1,128)S(1)}, f32[6,1,8,128]{3,1,2,0:T(1,128)S(1)}, u32[]{:S(2)}, u32[]{:S(2)}) collective-permute-start(f32[6,1,8,128]{3,1,2,0:T(1,128)S(1)} %get-tuple-element.43), channel_id=1, source_target_pairs={{0,8},{8,16},{16,24},{1,9},{9,17},{17,25},{2,10},{10,18},{18,26},{... | collective-permute-start | bytes 73736 | tf_op jit(solution)/shard_map/ppermute | solution.py:26
  38.7 1.6 %collective-permute-start.11 = (f32[6,32,10,1]{1,0,3,2:T(8,128)S(1)}, f32[6,32,10,1]{1,0,3,2:T(8,128)}, u32[]{:S(2)}, u32[]{:S(2)}) collective-permute-start(f32[6,32,10,1]{1,0,3,2:T(8,128)S(1)} %copy.61), channel_id=1, source_target_pairs={{0,1},{1,0},{2,3},{3,2},{4,5},{5,4},{6,7},{7,6},{8,9},{9,8},{10,11... | collective-permute-start | bytes 23048 | tf_op jit(solution)/shard_map/ppermute | solution.py:26
  40.3 1.4 %collective-permute-done.10 = f32[6,32,10,1]{1,0,3,2:T(8,128)S(1)} collective-permute-done((f32[6,32,10,1]{1,0,3,2:T(8,128)S(1)}, f32[6,32,10,1]{1,0,3,2:T(8,128)S(1)}, u32[]{:S(2)}, u32[]{:S(2)}) %collective-permute-start.10) | collective-permute-done | bytes 7712 | tf_op jit(solution)/shard_map/ppermute | solution.py:29
  48.1 3.8 %collective-permute-done.12 = f32[6,1,8,128]{3,1,2,0:T(1,128)S(1)} collective-permute-done((f32[6,1,8,128]{3,1,2,0:T(1,128)S(1)}, f32[6,1,8,128]{3,1,2,0:T(1,128)S(1)}, u32[]{:S(2)}, u32[]{:S(2)}) %collective-permute-start.12) | collective-permute-done | bytes 24608 | tf_op jit(solution)/shard_map/ppermute | solution.py:29
  52.0 2.4 %collective-permute-start.13 = (f32[6,1,8,128]{3,1,2,0:T(1,128)S(1)}, f32[6,1,8,128]{3,1,2,0:T(1,128)S(1)}, u32[]{:S(2)}, u32[]{:S(2)}) collective-permute-start(f32[6,1,8,128]{3,1,2,0:T(1,128)S(1)} %get-tuple-element.38), channel_id=1, source_target_pairs={{0,8},{8,16},{16,24},{1,9},{9,17},{17,25},{2,10},{10,18},{18,26},{... | collective-permute-start | bytes 73736 | tf_op jit(solution)/shard_map/ppermute | solution.py:26
  55.4 1.6 %collective-permute-start.16 = (f32[6,32,10,1]{1,0,3,2:T(8,128)S(1)}, f32[6,32,10,1]{1,0,3,2:T(8,128)S(1)}, u32[]{:S(2)}, u32[]{:S(2)}) collective-permute-start(f32[6,32,10,1]{1,0,3,2:T(8,128)S(1)} %copy.63), channel_id=1, source_target_pairs={{1,0},{0,1},{3,2},{2,3},{5,4},{4,5},{7,6},{6,7},{9,8},{8,9},{11,10... | collective-permute-start | bytes 23048 | tf_op jit(solution)/shard_map/ppermute | solution.py:29
  58.0 1.7 %collective-permute-done.16 = f32[6,32,10,1]{1,0,3,2:T(8,128)S(1)} collective-permute-done((f32[6,32,10,1]{1,0,3,2:T(8,128)S(1)}, f32[6,32,10,1]{1,0,3,2:T(8,128)S(1)}, u32[]{:S(2)}, u32[]{:S(2)}) %collective-permute-start.16) | collective-permute-done | bytes 7712 | tf_op jit(solution)/shard_map/ppermute | solution.py:29
  60.2 1.4 %collective-permute-done.17 = f32[6,32,10,1]{1,0,3,2:T(8,128)} collective-permute-done((f32[6,32,10,1]{1,0,3,2:T(8,128)S(1)}, f32[6,32,10,1]{1,0,3,2:T(8,128)}, u32[]{:S(2)}, u32[]{:S(2)}) %collective-permute-start.17) | collective-permute-done | bytes 7712 | tf_op jit(solution)/shard_map/ppermute | solution.py:26
  64.6 1.5 %collective-permute-start.18 = (f32[6,17,8,128]{3,2,1,0:T(8,128)S(1)}, f32[6,17,8,128]{3,2,1,0:T(8,128)S(1)}, u32[]{:S(2)}, u32[]{:S(2)}) collective-permute-start(f32[6,17,8,128]{3,2,1,0:T(8,128)S(1)} %copy.68), channel_id=1, source_target_pairs={{8,0},{16,8},{24,16},{9,1},{17,9},{25,17},{10,2},{18,10},{26,18},{... | collective-permute-start | bytes 1253384 | tf_op jit(solution)/shard_map/ppermute | solution.py:37
  66.6 9.7 %collective-permute-done.18 = f32[6,17,8,128]{3,2,1,0:T(8,128)S(1)} collective-permute-done((f32[6,17,8,128]{3,2,1,0:T(8,128)S(1)}, f32[6,17,8,128]{3,2,1,0:T(8,128)S(1)}, u32[]{:S(2)}, u32[]{:S(2)}) %collective-permute-start.18) | collective-permute-done | bytes 417824 | tf_op jit(solution)/shard_map/ppermute | solution.py:37
  77.2 2.4 %collective-permute-done.19 = f32[6,32,1,128]{3,1,2,0:T(8,128)S(1)} collective-permute-done((f32[6,32,1,128]{3,1,2,0:T(8,128)S(1)}, f32[6,32,1,128]{3,1,2,0:T(8,128)S(1)}, u32[]{:S(2)}, u32[]{:S(2)}) %collective-permute-start.19) | collective-permute-done | bytes 98336 | tf_op jit(solution)/shard_map/ppermute | solution.py:29
  82.1 1.7 %copy.71 = f32[6,32,10,1]{1,0,3,2:T(8,128)S(1)} copy(f32[6,32,10,1]{3,1,2,0:T(8,128)} %get-tuple-element.51) | data formatting | bytes 15360 | tf_op jit(solution)/shard_map/slice | solution.py:29
  89.2 1.4 %copy.74 = f32[6,32,10,1]{3,1,2,0:T(8,128)} copy(f32[6,32,10,1]{1,0,3,2:T(8,128)S(1)} %collective-permute-done.22) | data formatting | bytes 15360 | tf_op jit(solution)/shard_map/ppermute | solution.py:26
  90.6 1.9 %fusion.9 = f32[6,32,8,128]{3,1,2,0:T(8,128)S(1)} fusion(f32[6,16,8,128]{3,1,2,0:T(8,128)S(1)} %maximum_select_fusion, f32[6,16,8,128]{3,1,2,0:T(8,128)S(1)} %fusion.60, f32[6,32,10,1]{3,1,2,0:T(8,128)} %copy.74, f32[6,32,1,128]{3,1,2,0:T(8,128)S(1)} %collective-permute-done.19, f32[6,32,1,128]{3,1,2,0:T(8,128)S(1)} %collective-permute-done.20, ...), kind=kLoop, calls=%fused_computation.70 | loop fusion | flops 4718592 | bytes 1833984 | tf_op jit(solution)/shard_map/sub | solution.py:44
  95.3 3.8 %collective-permute-done.23 = f32[6,1,8,128]{3,1,2,0:T(1,128)S(1)} collective-permute-done((f32[6,1,8,128]{3,1,2,0:T(1,128)S(1)}, f32[6,1,8,128]{3,1,2,0:T(1,128)S(1)}, u32[]{:S(2)}, u32[]{:S(2)}) %collective-permute-start.23) | collective-permute-done | bytes 24608 | tf_op jit(solution)/shard_map/ppermute | solution.py:29
  99.2 4.2 %collective-permute-start.24 = (f32[6,1,8,128]{3,1,2,0:T(1,128)S(1)}, f32[6,1,8,128]{3,1,2,0:T(1,128)}, u32[]{:S(2)}, u32[]{:S(2)}) collective-permute-start(f32[6,1,8,128]{3,1,2,0:T(1,128)S(1)} %get-tuple-element.28), channel_id=1, source_target_pairs={{0,8},{8,16},{16,24},{1,9},{9,17},{17,25},{2,10},{10,18},{18,26},{... | collective-permute-start | bytes 73736 | tf_op jit(solution)/shard_map/ppermute | solution.py:26
  107.1 1.4 %collective-permute-done.27 = f32[6,32,10,1]{1,0,3,2:T(8,128)S(1)} collective-permute-done((f32[6,32,10,1]{1,0,3,2:T(8,128)S(1)}, f32[6,32,10,1]{1,0,3,2:T(8,128)S(1)}, u32[]{:S(2)}, u32[]{:S(2)}) %collective-permute-start.27) | collective-permute-done | bytes 7712 | tf_op jit(solution)/shard_map/ppermute | solution.py:29
  (164 shorter events, 50.9 us)
Async XLA Ops:
  2.6 6.8 %collective-permute-start = (f32[6,1,8,128]{3,1,2,0:T(1,128)S(1)}, f32[6,1,8,128]{3,1,2,0:T(1,128)S(1)}, u32[]{:S(2)}, u32[]{:S(2)}) collective-permute-start(f32[6,1,8,128]{3,1,2,0:T(1,128)S(1)} %fusion.99), channel_id=1, source_target_pairs={{8,0},{16,8},{24,16},{9,1},{17,9},{25,17},{10,2},{18,10},{26,18},{... | collective-permute-start | bytes 73736 | tf_op jit(solution)/shard_map/ppermute | solution.py:29
  4.0 10.6 %collective-permute-start.2 = (f32[6,32,1,128]{3,1,2,0:T(8,128)S(1)}, f32[6,32,1,128]{3,1,2,0:T(8,128)}, u32[]{:S(2)}, u32[]{:S(2)}) collective-permute-start(f32[6,32,1,128]{3,1,2,0:T(8,128)S(1)} %get-tuple-element.70), channel_id=1, source_target_pairs={{2,0},{4,2},{6,4},{0,6},{3,1},{5,3},{7,5},{1,7},{10,8},{12,10},{14... | collective-permute-start | bytes 294920 | tf_op jit(solution)/shard_map/ppermute | solution.py:29
  6.4 8.2 %collective-permute-start.3 = (f32[6,32,1,128]{3,1,2,0:T(8,128)S(1)}, f32[6,32,1,128]{3,1,2,0:T(8,128)}, u32[]{:S(2)}, u32[]{:S(2)}) collective-permute-start(f32[6,32,1,128]{3,1,2,0:T(8,128)S(1)} %get-tuple-element.69), channel_id=1, source_target_pairs={{0,2},{2,4},{4,6},{6,0},{1,3},{3,5},{5,7},{7,1},{8,10},{10,12},{12... | collective-permute-start | bytes 294920 | tf_op jit(solution)/shard_map/ppermute | solution.py:26
  10.1 9.7 %collective-permute-start.1 = (f32[6,1,8,128]{3,1,2,0:T(1,128)}, f32[6,1,8,128]{3,1,2,0:T(1,128)}, u32[]{:S(2)}, u32[]{:S(2)}) collective-permute-start(f32[6,1,8,128]{3,1,2,0:T(1,128)} %get-tuple-element.48), channel_id=1, source_target_pairs={{0,8},{8,16},{16,24},{1,9},{9,17},{17,25},{2,10},{10,18},{18,26},{... | collective-permute-start | bytes 73736 | tf_op jit(solution)/shard_map/ppermute | solution.py:26
  17.1 4.2 %collective-permute-start.4 = (f32[6,32,10,1]{1,0,3,2:T(8,128)}, f32[6,32,10,1]{1,0,3,2:T(8,128)S(1)}, u32[]{:S(2)}, u32[]{:S(2)}) collective-permute-start(f32[6,32,10,1]{1,0,3,2:T(8,128)} %copy.52), channel_id=1, source_target_pairs={{1,0},{0,1},{3,2},{2,3},{5,4},{4,5},{7,6},{6,7},{9,8},{8,9},{11,10... | collective-permute-start | bytes 23048 | tf_op jit(solution)/shard_map/ppermute | solution.py:29
  19.2 4.2 %collective-permute-start.5 = (f32[6,32,10,1]{1,0,3,2:T(8,128)S(1)}, f32[6,32,10,1]{1,0,3,2:T(8,128)}, u32[]{:S(2)}, u32[]{:S(2)}) collective-permute-start(f32[6,32,10,1]{1,0,3,2:T(8,128)S(1)} %copy.54), channel_id=1, source_target_pairs={{0,1},{1,0},{2,3},{3,2},{4,5},{5,4},{6,7},{7,6},{8,9},{9,8},{10,11... | collective-permute-start | bytes 23048 | tf_op jit(solution)/shard_map/ppermute | solution.py:26
  27.9 5.7 %collective-permute-start.6 = (f32[6,1,8,128]{3,1,2,0:T(1,128)S(1)}, f32[6,1,8,128]{3,1,2,0:T(1,128)S(1)}, u32[]{:S(2)}, u32[]{:S(2)}) collective-permute-start(f32[6,1,8,128]{3,1,2,0:T(1,128)S(1)} %fusion.97), channel_id=1, source_target_pairs={{8,0},{16,8},{24,16},{9,1},{17,9},{25,17},{10,2},{18,10},{26,18},{... | collective-permute-start | bytes 73736 | tf_op jit(solution)/shard_map/ppermute | solution.py:29
  29.2 7.4 %collective-permute-start.8 = (f32[6,32,1,128]{3,1,2,0:T(8,128)S(1)}, f32[6,32,1,128]{3,1,2,0:T(8,128)S(1)}, u32[]{:S(2)}, u32[]{:S(2)}) collective-permute-start(f32[6,32,1,128]{3,1,2,0:T(8,128)S(1)} %get-tuple-element.68), channel_id=1, source_target_pairs={{2,0},{4,2},{6,4},{0,6},{3,1},{5,3},{7,5},{1,7},{10,8},{12,10},{14... | collective-permute-start | bytes 294920 | tf_op jit(solution)/shard_map/ppermute | solution.py:29
  29.3 7.3 %collective-permute-start.9 = (f32[6,32,1,128]{3,1,2,0:T(8,128)S(1)}, f32[6,32,1,128]{3,1,2,0:T(8,128)S(1)}, u32[]{:S(2)}, u32[]{:S(2)}) collective-permute-start(f32[6,32,1,128]{3,1,2,0:T(8,128)S(1)} %get-tuple-element.67), channel_id=1, source_target_pairs={{0,2},{2,4},{4,6},{6,0},{1,3},{3,5},{5,7},{7,1},{8,10},{10,12},{12... | collective-permute-start | bytes 294920 | tf_op jit(solution)/shard_map/ppermute | solution.py:26
  33.7 6.6 %collective-permute-start.7 = (f32[6,1,8,128]{3,1,2,0:T(1,128)S(1)}, f32[6,1,8,128]{3,1,2,0:T(1,128)S(1)}, u32[]{:S(2)}, u32[]{:S(2)}) collective-permute-start(f32[6,1,8,128]{3,1,2,0:T(1,128)S(1)} %get-tuple-element.43), channel_id=1, source_target_pairs={{0,8},{8,16},{16,24},{1,9},{9,17},{17,25},{2,10},{10,18},{18,26},{... | collective-permute-start | bytes 73736 | tf_op jit(solution)/shard_map/ppermute | solution.py:26
  38.7 4.2 %collective-permute-start.11 = (f32[6,32,10,1]{1,0,3,2:T(8,128)S(1)}, f32[6,32,10,1]{1,0,3,2:T(8,128)}, u32[]{:S(2)}, u32[]{:S(2)}) collective-permute-start(f32[6,32,10,1]{1,0,3,2:T(8,128)S(1)} %copy.61), channel_id=1, source_target_pairs={{0,1},{1,0},{2,3},{3,2},{4,5},{5,4},{6,7},{7,6},{8,9},{9,8},{10,11... | collective-permute-start | bytes 23048 | tf_op jit(solution)/shard_map/ppermute | solution.py:26
  46.2 5.7 %collective-permute-start.12 = (f32[6,1,8,128]{3,1,2,0:T(1,128)S(1)}, f32[6,1,8,128]{3,1,2,0:T(1,128)S(1)}, u32[]{:S(2)}, u32[]{:S(2)}) collective-permute-start(f32[6,1,8,128]{3,1,2,0:T(1,128)S(1)} %fusion.95), channel_id=1, source_target_pairs={{8,0},{16,8},{24,16},{9,1},{17,9},{25,17},{10,2},{18,10},{26,18},{... | collective-permute-start | bytes 73736 | tf_op jit(solution)/shard_map/ppermute | solution.py:29
  47.6 6.8 %collective-permute-start.14 = (f32[6,32,1,128]{3,1,2,0:T(8,128)S(1)}, f32[6,32,1,128]{3,1,2,0:T(8,128)S(1)}, u32[]{:S(2)}, u32[]{:S(2)}) collective-permute-start(f32[6,32,1,128]{3,1,2,0:T(8,128)S(1)} %get-tuple-element.66), channel_id=1, source_target_pairs={{2,0},{4,2},{6,4},{0,6},{3,1},{5,3},{7,5},{1,7},{10,8},{12,10},{14... | collective-permute-start | bytes 294920 | tf_op jit(solution)/shard_map/ppermute | solution.py:29
  47.6 6.8 %collective-permute-start.15 = (f32[6,32,1,128]{3,1,2,0:T(8,128)S(1)}, f32[6,32,1,128]{3,1,2,0:T(8,128)S(1)}, u32[]{:S(2)}, u32[]{:S(2)}) collective-permute-start(f32[6,32,1,128]{3,1,2,0:T(8,128)S(1)} %get-tuple-element.65), channel_id=1, source_target_pairs={{0,2},{2,4},{4,6},{6,0},{1,3},{3,5},{5,7},{7,1},{8,10},{10,12},{12... | collective-permute-start | bytes 294920 | tf_op jit(solution)/shard_map/ppermute | solution.py:26
  52.0 6.0 %collective-permute-start.13 = (f32[6,1,8,128]{3,1,2,0:T(1,128)S(1)}, f32[6,1,8,128]{3,1,2,0:T(1,128)S(1)}, u32[]{:S(2)}, u32[]{:S(2)}) collective-permute-start(f32[6,1,8,128]{3,1,2,0:T(1,128)S(1)} %get-tuple-element.38), channel_id=1, source_target_pairs={{0,8},{8,16},{16,24},{1,9},{9,17},{17,25},{2,10},{10,18},{18,26},{... | collective-permute-start | bytes 73736 | tf_op jit(solution)/shard_map/ppermute | solution.py:26
  55.4 4.4 %collective-permute-start.16 = (f32[6,32,10,1]{1,0,3,2:T(8,128)S(1)}, f32[6,32,10,1]{1,0,3,2:T(8,128)S(1)}, u32[]{:S(2)}, u32[]{:S(2)}) collective-permute-start(f32[6,32,10,1]{1,0,3,2:T(8,128)S(1)} %copy.63), channel_id=1, source_target_pairs={{1,0},{0,1},{3,2},{2,3},{5,4},{4,5},{7,6},{6,7},{9,8},{8,9},{11,10... | collective-permute-start | bytes 23048 | tf_op jit(solution)/shard_map/ppermute | solution.py:29
  57.5 4.2 %collective-permute-start.17 = (f32[6,32,10,1]{1,0,3,2:T(8,128)S(1)}, f32[6,32,10,1]{1,0,3,2:T(8,128)}, u32[]{:S(2)}, u32[]{:S(2)}) collective-permute-start(f32[6,32,10,1]{1,0,3,2:T(8,128)S(1)} %copy.65), channel_id=1, source_target_pairs={{0,1},{1,0},{2,3},{3,2},{4,5},{5,4},{6,7},{7,6},{8,9},{9,8},{10,11... | collective-permute-start | bytes 23048 | tf_op jit(solution)/shard_map/ppermute | solution.py:26
  64.6 11.7 %collective-permute-start.18 = (f32[6,17,8,128]{3,2,1,0:T(8,128)S(1)}, f32[6,17,8,128]{3,2,1,0:T(8,128)S(1)}, u32[]{:S(2)}, u32[]{:S(2)}) collective-permute-start(f32[6,17,8,128]{3,2,1,0:T(8,128)S(1)} %copy.68), channel_id=1, source_target_pairs={{8,0},{16,8},{24,16},{9,1},{17,9},{25,17},{10,2},{18,10},{26,18},{... | collective-permute-start | bytes 1253384 | tf_op jit(solution)/shard_map/ppermute | solution.py:37
  76.6 4.1 %collective-permute-start.20 = (f32[6,32,1,128]{3,1,2,0:T(8,128)S(1)}, f32[6,32,1,128]{3,1,2,0:T(8,128)S(1)}, u32[]{:S(2)}, u32[]{:S(2)}) collective-permute-start(f32[6,32,1,128]{3,1,2,0:T(8,128)S(1)} %get-tuple-element.61), channel_id=1, source_target_pairs={{0,2},{2,4},{4,6},{6,0},{1,3},{3,5},{5,7},{7,1},{8,10},{10,12},{12... | collective-permute-start | bytes 294920 | tf_op jit(solution)/shard_map/ppermute | solution.py:26
  93.4 5.7 %collective-permute-start.23 = (f32[6,1,8,128]{3,1,2,0:T(1,128)S(1)}, f32[6,1,8,128]{3,1,2,0:T(1,128)S(1)}, u32[]{:S(2)}, u32[]{:S(2)}) collective-permute-start(f32[6,1,8,128]{3,1,2,0:T(1,128)S(1)} %fusion.93), channel_id=1, source_target_pairs={{8,0},{16,8},{24,16},{9,1},{17,9},{25,17},{10,2},{18,10},{26,18},{... | collective-permute-start | bytes 73736 | tf_op jit(solution)/shard_map/ppermute | solution.py:29
  94.8 8.7 %collective-permute-start.25 = (f32[6,32,1,128]{3,1,2,0:T(8,128)S(1)}, f32[6,32,1,128]{3,1,2,0:T(8,128)S(1)}, u32[]{:S(2)}, u32[]{:S(2)}) collective-permute-start(f32[6,32,1,128]{3,1,2,0:T(8,128)S(1)} %get-tuple-element.60), channel_id=1, source_target_pairs={{2,0},{4,2},{6,4},{0,6},{3,1},{5,3},{7,5},{1,7},{10,8},{12,10},{14... | collective-permute-start | bytes 294920 | tf_op jit(solution)/shard_map/ppermute | solution.py:29
  94.8 8.6 %collective-permute-start.26 = (f32[6,32,1,128]{3,1,2,0:T(8,128)S(1)}, f32[6,32,1,128]{3,1,2,0:T(8,128)S(1)}, u32[]{:S(2)}, u32[]{:S(2)}) collective-permute-start(f32[6,32,1,128]{3,1,2,0:T(8,128)S(1)} %get-tuple-element.59), channel_id=1, source_target_pairs={{0,2},{2,4},{4,6},{6,0},{1,3},{3,5},{5,7},{7,1},{8,10},{10,12},{12... | collective-permute-start | bytes 294920 | tf_op jit(solution)/shard_map/ppermute | solution.py:26
  99.2 7.9 %collective-permute-start.24 = (f32[6,1,8,128]{3,1,2,0:T(1,128)S(1)}, f32[6,1,8,128]{3,1,2,0:T(1,128)}, u32[]{:S(2)}, u32[]{:S(2)}) collective-permute-start(f32[6,1,8,128]{3,1,2,0:T(1,128)S(1)} %get-tuple-element.28), channel_id=1, source_target_pairs={{0,8},{8,16},{16,24},{1,9},{9,17},{17,25},{2,10},{10,18},{18,26},{... | collective-permute-start | bytes 73736 | tf_op jit(solution)/shard_map/ppermute | solution.py:26
  106.0 4.2 %collective-permute-start.28 = (f32[6,32,10,1]{1,0,3,2:T(8,128)S(1)}, f32[6,32,10,1]{1,0,3,2:T(8,128)}, u32[]{:S(2)}, u32[]{:S(2)}) collective-permute-start(f32[6,32,10,1]{1,0,3,2:T(8,128)S(1)} %copy.77), channel_id=1, source_target_pairs={{0,1},{1,0},{2,3},{3,2},{4,5},{5,4},{6,7},{7,6},{8,9},{9,8},{10,11... | collective-permute-start | bytes 23048 | tf_op jit(solution)/shard_map/ppermute | solution.py:26
  (16 other events, 96.8 us)
where the time goes:
time: 116 us; the launch traced here: 115 us
  waiting for transfers between devices  40.2 us (35%)
  starting transfers between devices  35.9 us (31%)
  local copies, waits for them, and re-layouts  24 us (21%)
  other arithmetic  13.6 us (12%)
  between operations  1.43 us (1%)
    ppermute x14, waiting for transfers between devices, with_halo(): lax.ppermute(lax.slice_in_dim(block, 0, width, axis=dim), axis, backward)  23.6 us
    ppermute x14, starting transfers between devices, with_halo(): lax.ppermute(lax.slice_in_dim(block, block.shape[dim] - width, None, axis...  21.1 us
    ppermute x14, starting transfers between devices, with_halo(): lax.ppermute(lax.slice_in_dim(block, 0, width, axis=dim), axis, backward)  13.3 us
    ppermute x1, waiting for transfers between devices, shifted_2(): lax.ppermute(value, axis, [(source, source + steps) for source in range(f...  9.69 us
    slice x10, local copies, waits for them, and re-layouts, with_halo(): lax.slice_in_dim(block, 0, width, axis=dim)  7.19 us
    ppermute x14, waiting for transfers between devices, with_halo(): lax.ppermute(lax.slice_in_dim(block, block.shape[dim] - width, None, axis...  6.93 us
    ppermute x5, local copies, waits for them, and re-layouts, with_halo(): lax.ppermute(lax.slice_in_dim(block, block.shape[dim] - width, None, axis...  6.21 us
    sub x5, other arithmetic, laplacian(): return total - 6.0 * fields  5.56 us
  transfers between devices with their start and end apart: 29, of which 17 were waited for; matrix products, arithmetic and copies ran while one was open for 11% of the time, Pallas kernels for 0%

commit v1 on v0

v1 whole, which is shorter than its diff:
```python
import functools

import jax
import jax.numpy as jnp
from jax import lax
from jax.experimental import pallas as pl
from jax.experimental.pallas import tpu as pltpu
from jax.sharding import PartitionSpec as P

STEPS_BEFORE = 3
STEPS_AFTER = 2
STEPS = STEPS_BEFORE + STEPS_AFTER
HALF = 7
WIDE = 2 * HALF
MESH = pl.DeviceIdType.MESH


class Plan:
    def __init__(self, planes, rows, shift):
        self.planes, self.rows, self.shift = planes, rows, shift
        self.skip = (shift - STEPS) // 8 * 8
        self.own = planes - self.skip
        self.above = shift + STEPS
        self.upper = -(-self.above // 8) * 8
        self.deep = self.own + self.upper
        self.first = shift - self.skip
        self.start = self.first - STEPS + 1
        self.tiles = -(-(planes + 2 * (STEPS - 1)) // 8)
        self.tall = rows + 2 * STEPS
        self.slots = self.tall // 2


def gather_kernel(plan, mesh_shape, levels, lab, pot, codes, table, main, strip, lab_up, pot_up, pack, g_send, g_recv, y_send, y_recv, z_send, z_recv):
    g, y, z = lax.axis_index("grow"), lax.axis_index("gy"), lax.axis_index("gz")
    count_g, count_y, count_z = mesh_shape
    rows, own, tall = plan.rows, plan.own, plan.tall
    has_below, has_above = g > 0, g < count_g - 1
    y_up, y_down = lax.rem(y + 1, count_y), lax.rem(y + count_y - 1, count_y)
    z_other = lax.rem(z + 1, count_z)

    barrier = pltpu.get_barrier_semaphore()

    def greet(target):
        pl.semaphore_signal(barrier, inc=1, device_id=target, device_id_type=MESH)

    @pl.when(has_below)
    def _():
        greet((g - 1, y, z))

    @pl.when(has_above)
    def _():
        greet((g + 1, y, z))

    greet((g, y_up, z))
    greet((g, y_down, z))
    greet((g, y, z_other))
    pl.semaphore_wait(barrier, 3 + has_below.astype(jnp.int32) + has_above.astype(jnp.int32))

    def g_copy(i):
        size = plan.above * rows
        src = lab.at[pl.ds(0, size)] if i == 0 else pot.at[i - 1, pl.ds(0, size)]
        dst = lab_up if i == 0 else pot_up.at[i - 1]
        return pltpu.make_async_remote_copy(
            src_ref=src, dst_ref=dst, send_sem=g_send.at[i], recv_sem=g_recv.at[i],
            device_id=(g - 1, y, z), device_id_type=MESH)

    @pl.when(has_below)
    def _():
        for i in range(3):
            g_copy(i).start()

    def y_copy(slot, values, low, size, up):
        if up:
            src, dst, target = rows, 0, y_up
        else:
            src, dst, target = STEPS, STEPS + rows, y_down
        return pltpu.make_async_remote_copy(
            src_ref=main.at[values, pl.ds(src, STEPS), pl.ds(low, size)],
            dst_ref=main.at[values, pl.ds(dst, STEPS), pl.ds(low, size)],
            send_sem=y_send.at[slot], recv_sem=y_recv.at[slot],
            device_id=(g, target, z), device_id_type=MESH)

    def row_of(ref, i, row, begin, size):
        at = pl.ds(begin * rows + row, size, stride=rows)
        return ref[at].astype(jnp.float32) if i == 0 else ref[i - 1, at]

    own_copies = []
    for i in range(3):
        for row in range(rows):
            main[i, STEPS + row, 0:own] = row_of(lab if i == 0 else pot, i, row, plan.skip, own)
        for up in (True, False):
            copy = y_copy(2 * i + up, i, 0, own, up)
            copy.start()
            own_copies.append(copy)

    up_copies = []
    for i in range(3):
        @pl.when(has_above)
        def _(i=i):
            g_copy(i).wait_recv()
            for row in range(rows):
                main[i, STEPS + row, own : own + plan.above] = row_of(lab_up if i == 0 else pot_up, i, row, 0, plan.above)
                rest = plan.upper - plan.above
                if rest:
                    main[i, STEPS + row, own + plan.above : plan.deep] = jnp.zeros((rest, 128), jnp.float32)

        @pl.when(jnp.logical_not(has_above))
        def _(i=i):
            for row in range(rows):
                if i == 0:
                    main[0, STEPS + row, own : own + plan.shift] = jnp.full((plan.shift, 128), 3.0, jnp.float32)
                else:
                    code = codes[pl.ds(row, plan.shift, stride=rows)]
                    value = jnp.zeros((plan.shift, 128), jnp.float32)
                    for level in range(levels):
                        value = jnp.where(code == level, table[i - 1, level], value)
                    main[i, STEPS + row, own : own + plan.shift] = value
                left = plan.deep - own - plan.shift
                main[i, STEPS + row, own + plan.shift : plan.deep] = jnp.zeros((left, 128), jnp.float32)

        for up in (True, False):
            copy = y_copy(6 + 2 * i + up, i, own, plan.upper, up)
            copy.start()
            up_copies.append(copy)

    lane = lax.broadcasted_iota(jnp.int32, (plan.deep, 128), 1)
    z_copies = []
    for i in range(3):
        for copy in own_copies[2 * i : 2 * i + 2] + up_copies[2 * i : 2 * i + 2]:
            copy.wait_recv()
        for parity in range(2):
            packed = jnp.zeros((plan.deep, 128), jnp.float32)
            for slot in range(plan.slots):
                turned = pltpu.roll(main[i, 2 * slot + parity], WIDE * slot + HALF, 1)
                inside = (lane >= WIDE * slot) & (lane < WIDE * slot + WIDE)
                packed = jnp.where(inside, turned, packed)
            pack[i, parity] = packed
        copy = pltpu.make_async_remote_copy(
            src_ref=pack.at[i], dst_ref=strip.at[i], send_sem=z_send.at[i], recv_sem=z_recv.at[i],
            device_id=(g, y, z_other), device_id_type=MESH)
        copy.start()
        z_copies.append(copy)

    for copy in z_copies:
        copy.wait()
    for copy in own_copies + up_copies:
        copy.wait_send()

    @pl.when(has_below)
    def _():
        for i in range(3):
            g_copy(i).wait_send()


def cell_step(center, laplace):
    p, (m0, m1) = center[:4], center[4:]
    both = m0 + m1
    third = 0.3 * both + 0.15
    minus_w = (third + 2.1 * m0, third + 2.1 * m1, third, 1.05 * both)
    squares = [v * v for v in p]
    total = (squares[0] + squares[1]) + (squares[2] + squares[3])
    scaled = 0.6 * total
    raw = []
    for a in range(4):
        inner = (1.0 - p[a]) * minus_w[a] - (scaled - 0.6 * squares[a])
        raw.append(0.12 * laplace[a] + p[a] * inner)
    mean = 0.25 * ((raw[0] + raw[1]) + (raw[2] + raw[3]))
    held = [jnp.clip(p[a] + (raw[a] - mean), 0.0, 1.0) for a in range(4)]
    inverse = 1.0 / ((held[0] + held[1]) + (held[2] + held[3]))
    new = [v * inverse for v in held]
    change = [new[a] * new[a] * (3.0 - 2.0 * new[a]) - squares[a] * (3.0 - 2.0 * p[a]) for a in range(4)]
    shared = 0.1 * (change[0] + change[1] + change[2]) + 0.35 * change[3]
    mobility = 0.15 * (0.05 * (p[0] + p[1] + p[2]) + p[3])
    new0 = m0 + mobility * laplace[4] - (shared + 0.7 * change[0])
    new1 = m1 + mobility * laplace[5] - (shared + 0.7 * change[1])
    return new + [new0, new1]


def steps_kernel(plan, count_g, main0, strip0, phases, potentials, main_a, main_b, strip_a, strip_b):
    g = lax.axis_index("grow")
    is_first, is_last = g == 0, g == count_g - 1
    rows, tall, deep = plan.rows, plan.tall, plan.deep

    def unpack(source, target, index):
        label = source[(0,) + index]
        for a in range(4):
            target[(a,) + index] = jnp.where(label == float(a), 1.0, 0.0)
        for i in range(2):
            target[(4 + i,) + index] = source[(1 + i,) + index]

    def unpack_row(row, carry):
        unpack(main0, main_a, (row,))
        return carry

    lax.fori_loop(0, tall, unpack_row, 0)
    for parity in range(2):
        unpack(strip0, strip_a, (parity,))

    lane = lax.broadcasted_iota(jnp.int32, (8, 128), 1)
    place = lax.broadcasted_iota(jnp.int32, (8, 128), 0)
    at_left, at_right = lane == 0, lane == 127
    inner_left, inner_right = lane % WIDE == HALF - 1, lane % WIDE == HALF

    def grow_sides(ref, index, low, center, top, bottom):
        above = ref[index + (pl.ds(low + 1, 8), slice(None))]
        below = ref[index + (pl.ds(low - 1, 8), slice(None))]
        if top is not None and low <= top < low + 8:
            above = jnp.where((place == top - low) & is_last, center, above)
        if bottom is not None and low <= bottom < low + 8:
            below = jnp.where((place == bottom - low) & is_first, center, below)
        return above + below

    def main_tile(src, strips, row, low, top, bottom):
        slot, parity = row // 2, lax.rem(row, 2)
        turn = 128 - (WIDE * slot + HALF)
        center, laplace = [], []
        for f in range(6):
            v = src[f, row, pl.ds(low, 8), :]
            near = pltpu.roll(strips[f, parity, pl.ds(low, 8), :], turn, 1)
            right = pltpu.roll(jnp.where(at_left, near, v), 127, 1)
            left = pltpu.roll(jnp.where(at_right, near, v), 1, 1)
            total = grow_sides(src, (f, row), low, v, top, bottom)
            total = total + (src[f, row + 1, pl.ds(low, 8), :] + src[f, row - 1, pl.ds(low, 8), :])
            total = total + (right + left)
            center.append(v)
            laplace.append(total - 6.0 * v)
        return cell_step(center, laplace)

    def strip_tile(src, strips, parity, low, top, bottom):
        center, laplace = [], []
        for f in range(6):
            v = strips[f, parity, pl.ds(low, 8), :]
            edge = jnp.zeros((8, 128), jnp.float32)
            for slot in range(plan.slots):
                turned = pltpu.roll(src[f, 2 * slot + parity, pl.ds(low, 8), :], WIDE * slot + HALF, 1)
                edge = jnp.where((lane >= WIDE * slot) & (lane < WIDE * slot + WIDE), turned, edge)
            right = jnp.where(inner_left, pltpu.roll(edge, 127, 1), pltpu.roll(v, 127, 1))
            left = jnp.where(inner_right, pltpu.roll(edge, 1, 1), pltpu.roll(v, 1, 1))
            other = strips[f, 1 - parity, pl.ds(low, 8), :]
            across = pltpu.roll(other, WIDE if parity == 0 else 128 - WIDE, 1)
            total = grow_sides(strips, (f, parity), low, v, top, bottom)
            total = total + (other + across) + (right + left)
            center.append(v)
            laplace.append(total - 6.0 * v)
        return cell_step(center, laplace)

    state = (main_a, strip_a, main_b, strip_b)
    for step in range(1, STEPS + 1):
        src, strips, dst, strips_dst = state
        early = step <= STEPS_BEFORE
        top = plan.own - 1 if early else plan.first + plan.planes - 1
        bottom = None if early else plan.first
        if step < STEPS:
            def row_step(row, carry):
                for tile in range(plan.tiles):
                    low = plan.start + 8 * tile
                    new = main_tile(src, strips, row, low, top, bottom)
                    for f in range(6):
                        dst[f, row, pl.ds(low, 8), :] = new[f]
                return carry

            lax.fori_loop(step, tall - step, row_step, 0)
            for tile in range(plan.tiles):
                for parity in range(2):
                    low = plan.start + 8 * tile
                    new = strip_tile(src, strips, parity, low, top, bottom)
                    for f in range(6):
                        strips_dst[f, parity, pl.ds(low, 8), :] = new[f]
        else:
            def row_last(row, carry):
                for tile in range(plan.planes // 8):
                    low = plan.first + 8 * tile
                    new = main_tile(src, strips, row + STEPS, low, top, bottom)
                    at = pl.ds(8 * tile * rows + row, 8, stride=rows)
                    for f in range(4):
                        phases[f, at, :] = new[f]
                    for i in range(2):
                        potentials[i, at, :] = new[4 + i]
                return carry

            lax.fori_loop(0, rows, row_last, 0)
        if step == STEPS_BEFORE:
            melt = (slice(plan.own, plan.own + plan.shift), slice(None))

            @pl.when(is_last)
            def _():
                def fill(row, carry):
                    unpack(main0, dst, (row,) + melt)
                    return carry

                lax.fori_loop(0, tall, fill, 0)
                for parity in range(2):
                    unpack(strip0, strips_dst, (parity,) + melt)

        state = (dst, strips_dst, src, strips)


def on_device(mesh_shape, labels, potential, melt_codes, melt_table):
    planes, rows, width = labels.shape
    shift, levels = melt_codes.shape[0], melt_table.shape[1]
    plan = Plan(planes, rows, shift)
    flat = planes * rows
    vmem = pl.BlockSpec(memory_space=pltpu.VMEM)
    smem = pl.BlockSpec(memory_space=pltpu.SMEM)
    f32 = jnp.float32
    dma = pltpu.SemaphoreType.DMA
    main0, strip0 = pl.pallas_call(
        functools.partial(gather_kernel, plan, mesh_shape, levels),
        out_shape=(
            jax.ShapeDtypeStruct((3, plan.tall, plan.deep, width), f32),
            jax.ShapeDtypeStruct((3, 2, plan.deep, width), f32),
        ),
        in_specs=[vmem, vmem, vmem, smem],
        out_specs=(vmem, vmem),
        scratch_shapes=[
            pltpu.VMEM((plan.above * rows, width), jnp.int32),
            pltpu.VMEM((2, plan.above * rows, width), f32),
            pltpu.VMEM((3, 2, plan.deep, width), f32),
            dma((3,)), dma((3,)), dma((12,)), dma((12,)), dma((3,)), dma((3,)),
        ],
        compiler_params=pltpu.CompilerParams(collective_id=0, has_side_effects=True),
        name="gather",
    )(labels.reshape(flat, width), potential.reshape(2, flat, width), melt_codes.reshape(shift * rows, width), melt_table)
    phases, potentials = pl.pallas_call(
        functools.partial(steps_kernel, plan, mesh_shape[0]),
        out_shape=(
            jax.ShapeDtypeStruct((4, flat, width), f32),
            jax.ShapeDtypeStruct((2, flat, width), f32),
        ),
        in_specs=[vmem, vmem],
        out_specs=(vmem, vmem),
        scratch_shapes=[
            pltpu.VMEM((6, plan.tall, plan.deep, width), f32),
            pltpu.VMEM((6, plan.tall, plan.deep, width), f32),
            pltpu.VMEM((6, 2, plan.deep, width), f32),
            pltpu.VMEM((6, 2, plan.deep, width), f32),
        ],
        name="steps",
    )(main0, strip0)
    return phases.reshape(4, planes, rows, width), potentials.reshape(2, planes, rows, width)


def solution(mesh):
    mesh_shape = tuple(mesh.shape[axis] for axis in ("grow", "gy", "gz"))
    return jax.shard_map(
        functools.partial(on_device, mesh_shape),
        mesh=mesh,
        in_specs=(P("grow", "gy", "gz"), P(None, "grow", "gy", "gz"), P(None, "gy", "gz"), P()),
        out_specs=(P(None, "grow", "gy", "gz"), P(None, "grow", "gy", "gz")),
        check_vma=False,
    )
```

time: 116 us -> 53.3 us (0.46)
  Pallas kernels: 0 us -> 52.3 us
  waiting for transfers between devices: 40.2 us -> 0 us
  starting transfers between devices: 35.9 us -> 0 us
  local copies, waits for them, and re-layouts: 24 us -> 0 us
  other arithmetic: 13.6 us -> 0 us
    pallas_call x0 -> x2, Pallas kernels: none -> 52.3 us  [the longest x1 33.2 us: on_device(): pl.pallas_call(functools.partial(steps_kernel, plan, mesh_shape[0]), out_...]
    ppermute x29 -> x0, waiting for transfers between devices: 40.2 us -> none  [the longest x14 23.6 us: with_halo(): lax.ppermute(lax.slice_in_dim(block, 0, width, axis=dim), axis, backward)]
    ppermute x29 -> x0, starting transfers between devices: 35.9 us -> none  [the longest x14 21.1 us: with_halo(): lax.ppermute(lax.slice_in_dim(block, block.shape[dim] - width, None, axis...]
    slice x18 -> x0, local copies, waits for them, and re-layouts: 9.96 us -> none  [the longest x10 7.19 us: with_halo(): lax.slice_in_dim(block, 0, width, axis=dim)]
    ppermute x10 -> x0, local copies, waits for them, and re-layouts: 8.37 us -> none  [the longest x5 6.21 us: with_halo(): lax.ppermute(lax.slice_in_dim(block, block.shape[dim] - width, None, axis...]
    sub x10 -> x0, other arithmetic: 5.96 us -> none  [the longest x5 5.56 us: laplacian(): return total - 6.0 * fields]
    unnamed x26 -> x0, local copies, waits for them, and re-layouts: 5.45 us -> none
    reduce_sum x17 -> x0, other arithmetic: 4.12 us -> none  [the longest x5 1.84 us: advance(): jnp.sum(change * comp_first, axis=0, keepdims=True)]
  transfers between devices with their start and end apart: 29 -> 0, of which waited for: 17 -> 0; matrix products, arithmetic and copies ran while one was open for 11% -> 0% of each run, Pallas kernels for 0% -> 0%
where the time goes in v1:
time: 53.3 us; the launch traced here: 52.9 us
  Pallas kernels  52.3 us (98%)
  between operations  0.64 us (1%)
    pallas_call x1, Pallas kernels, on_device(): pl.pallas_call(functools.partial(steps_kernel, plan, mesh_shape[0]), out_...  33.2 us
    pallas_call x1, Pallas kernels, on_device(): pl.pallas_call(functools.partial(gather_kernel, plan, mesh_shape, levels)...  19.1 us

profile of v1, /device:TPU:0, one launch (start us, length us, event | category | flops | bytes accessed | tf_op | source)
XLA Modules:
  0.0 52.9 jit_solution(3418448480787874958)
XLA Ops:
  0.6 19.1 %gather.1 = (f32[3,18,48,128]{3,2,1,0:T(8,128)}, f32[3,2,48,128]{3,2,1,0:T(8,128)}) custom-call(s32[256,128]{1,0:T(8,128)} %bitcast.6, f32[2,256,128]{2,1,0:T(8,128)} %bitcast.5, s32[128,128]{1,0:T(8,128)} %bitcast.7, f32[2,8]{1,0:T(2,128)} %table.1), custom_call_target="tpu_custom_call" | custom-call | tf_op jit(solution)/shard_map/gather/pallas_call | solution.py:307
  19.8 33.2 %steps.1 = (f32[4,256,128]{2,1,0:T(8,128)}, f32[2,256,128]{2,1,0:T(8,128)}) custom-call(f32[3,18,48,128]{3,2,1,0:T(8,128)} %get-tuple-element.6.main0, f32[3,2,48,128]{3,2,1,0:T(8,128)} %get-tuple-element.7.strip0), custom_call_target="tpu_custom_call" | custom-call | tf_op jit(solution)/shard_map/steps/pallas_call | solution.py:324

commit v2 on v1

--- a/solution.py
+++ b/solution.py
@@ -30,7 +30,7 @@
         self.slots = self.tall // 2
 
 
-def gather_kernel(plan, mesh_shape, levels, lab, pot, codes, table, main, strip, lab_up, pot_up, pack, g_send, g_recv, y_send, y_recv, z_send, z_recv):
+def gather_kernel(plan, mesh_shape, levels, lab, pot, codes, table, main, strip, pack, lab_up, pot_up, g_send, g_recv, y_send, y_recv, z_send, z_recv):
     g, y, z = lax.axis_index("grow"), lax.axis_index("gy"), lax.axis_index("gz")
     count_g, count_y, count_z = mesh_shape
     rows, own, tall = plan.rows, plan.own, plan.tall
@@ -152,31 +152,27 @@
             g_copy(i).wait_send()
 
 
-def cell_step(center, laplace):
+def cell_step(center, sums):
     p, (m0, m1) = center[:4], center[4:]
-    both = m0 + m1
-    third = 0.3 * both + 0.15
-    minus_w = (third + 2.1 * m0, third + 2.1 * m1, third, 1.05 * both)
+    around = sums[:3] + [6.0 - (sums[0] + sums[1] + sums[2])]
+    third = 0.3 * (m0 + m1) + 0.15
+    minus_w = (third + 2.1 * m0, third + 2.1 * m1, third, 3.5 * third - 0.525)
     squares = [v * v for v in p]
-    total = (squares[0] + squares[1]) + (squares[2] + squares[3])
-    scaled = 0.6 * total
-    raw = []
-    for a in range(4):
-        inner = (1.0 - p[a]) * minus_w[a] - (scaled - 0.6 * squares[a])
-        raw.append(0.12 * laplace[a] + p[a] * inner)
-    mean = 0.25 * ((raw[0] + raw[1]) + (raw[2] + raw[3]))
-    held = [jnp.clip(p[a] + (raw[a] - mean), 0.0, 1.0) for a in range(4)]
+    shared = 0.28 - 0.6 * ((squares[0] + squares[1]) + (squares[2] + squares[3]))
+    local = [p[a] * ((shared + minus_w[a]) + p[a] * (0.6 * p[a] - minus_w[a])) for a in range(4)]
+    mean = 0.25 * ((local[0] + local[1]) + (local[2] + local[3])) - 0.07
+    held = [jnp.clip((0.12 * around[a] - mean) + local[a], 0.0, 1.0) for a in range(4)]
     inverse = 1.0 / ((held[0] + held[1]) + (held[2] + held[3]))
     new = [v * inverse for v in held]
-    change = [new[a] * new[a] * (3.0 - 2.0 * new[a]) - squares[a] * (3.0 - 2.0 * p[a]) for a in range(4)]
-    shared = 0.1 * (change[0] + change[1] + change[2]) + 0.35 * change[3]
-    mobility = 0.15 * (0.05 * (p[0] + p[1] + p[2]) + p[3])
-    new0 = m0 + mobility * laplace[4] - (shared + 0.7 * change[0])
-    new1 = m1 + mobility * laplace[5] - (shared + 0.7 * change[1])
+    change = [new[a] * new[a] * (1.5 - new[a]) - squares[a] * (1.5 - p[a]) for a in range(4)]
+    release = 0.2 * (change[0] + change[1] + change[2]) + 0.7 * change[3]
+    mobility = 0.0075 + 0.1425 * p[3]
+    new0 = (m0 + mobility * (sums[3] - 6.0 * m0)) - (release + 1.4 * change[0])
+    new1 = (m1 + mobility * (sums[4] - 6.0 * m1)) - (release + 1.4 * change[1])
     return new + [new0, new1]
 
 
-def steps_kernel(plan, count_g, main0, strip0, phases, potentials, main_a, main_b, strip_a, strip_b):
+def steps_kernel(plan, count_g, main0, strip0, edge0, phases, potentials, main_a, main_b, strip_a, strip_b, edges):
     g = lax.axis_index("grow")
     is_first, is_last = g == 0, g == count_g - 1
     rows, tall, deep = plan.rows, plan.tall, plan.deep
@@ -195,6 +191,7 @@
     lax.fori_loop(0, tall, unpack_row, 0)
     for parity in range(2):
         unpack(strip0, strip_a, (parity,))
+        unpack(edge0, edges, (parity,))
 
     lane = lax.broadcasted_iota(jnp.int32, (8, 128), 1)
     place = lax.broadcasted_iota(jnp.int32, (8, 128), 0)
@@ -210,39 +207,36 @@
             below = jnp.where((place == bottom - low) & is_first, center, below)
         return above + below
 
+    moving = (0, 1, 2, 4, 5)
+
     def main_tile(src, strips, row, low, top, bottom):
         slot, parity = row // 2, lax.rem(row, 2)
         turn = 128 - (WIDE * slot + HALF)
-        center, laplace = [], []
-        for f in range(6):
-            v = src[f, row, pl.ds(low, 8), :]
+        center = [src[f, row, pl.ds(low, 8), :] for f in range(6)]
+        sums = []
+        for f in moving:
+            v = center[f]
             near = pltpu.roll(strips[f, parity, pl.ds(low, 8), :], turn, 1)
             right = pltpu.roll(jnp.where(at_left, near, v), 127, 1)
             left = pltpu.roll(jnp.where(at_right, near, v), 1, 1)
             total = grow_sides(src, (f, row), low, v, top, bottom)
             total = total + (src[f, row + 1, pl.ds(low, 8), :] + src[f, row - 1, pl.ds(low, 8), :])
-            total = total + (right + left)
-            center.append(v)
-            laplace.append(total - 6.0 * v)
-        return cell_step(center, laplace)
-
-    def strip_tile(src, strips, parity, low, top, bottom):
-        center, laplace = [], []
-        for f in range(6):
-            v = strips[f, parity, pl.ds(low, 8), :]
-            edge = jnp.zeros((8, 128), jnp.float32)
-            for slot in range(plan.slots):
-                turned = pltpu.roll(src[f, 2 * slot + parity, pl.ds(low, 8), :], WIDE * slot + HALF, 1)
-                edge = jnp.where((lane >= WIDE * slot) & (lane < WIDE * slot + WIDE), turned, edge)
-            right = jnp.where(inner_left, pltpu.roll(edge, 127, 1), pltpu.roll(v, 127, 1))
-            left = jnp.where(inner_right, pltpu.roll(edge, 1, 1), pltpu.roll(v, 1, 1))
+            sums.append(total + (right + left))
+        return cell_step(center, sums)
+
+    def strip_tile(strips, parity, low, top, bottom):
+        center = [strips[f, parity, pl.ds(low, 8), :] for f in range(6)]
+        sums = []
+        for f in moving:
+            v = center[f]
+            edge = edges[f, parity, pl.ds(low, 8), :]
+            right = pltpu.roll(jnp.where(inner_right, edge, v), 127, 1)
+            left = pltpu.roll(jnp.where(inner_left, edge, v), 1, 1)
             other = strips[f, 1 - parity, pl.ds(low, 8), :]
             across = pltpu.roll(other, WIDE if parity == 0 else 128 - WIDE, 1)
             total = grow_sides(strips, (f, parity), low, v, top, bottom)
-            total = total + (other + across) + (right + left)
-            center.append(v)
-            laplace.append(total - 6.0 * v)
-        return cell_step(center, laplace)
+            sums.append(total + (other + across) + (right + left))
+        return cell_step(center, sums)
 
     state = (main_a, strip_a, main_b, strip_b)
     for step in range(1, STEPS + 1):
@@ -251,21 +245,28 @@
         top = plan.own - 1 if early else plan.first + plan.planes - 1
         bottom = None if early else plan.first
         if step < STEPS:
+            for tile in range(plan.tiles):
+                for parity in range(2):
+                    low = plan.start + 8 * tile
+                    new = strip_tile(strips, parity, low, top, bottom)
+                    for f in range(6):
+                        strips_dst[f, parity, pl.ds(low, 8), :] = new[f]
+
             def row_step(row, carry):
+                slot, parity = row // 2, lax.rem(row, 2)
+                turn = WIDE * slot + HALF
+                inside = (lane == turn) | (lane == turn - 1)
                 for tile in range(plan.tiles):
                     low = plan.start + 8 * tile
                     new = main_tile(src, strips, row, low, top, bottom)
                     for f in range(6):
                         dst[f, row, pl.ds(low, 8), :] = new[f]
+                        if f in moving and step < STEPS - 1:
+                            at = (f, parity, pl.ds(low, 8), slice(None))
+                            edges[at] = jnp.where(inside, pltpu.roll(new[f], turn, 1), edges[at])
                 return carry
 
             lax.fori_loop(step, tall - step, row_step, 0)
-            for tile in range(plan.tiles):
-                for parity in range(2):
-                    low = plan.start + 8 * tile
-                    new = strip_tile(src, strips, parity, low, top, bottom)
-                    for f in range(6):
-                        strips_dst[f, parity, pl.ds(low, 8), :] = new[f]
         else:
             def row_last(row, carry):
                 for tile in range(plan.planes // 8):
@@ -291,6 +292,7 @@
                 lax.fori_loop(0, tall, fill, 0)
                 for parity in range(2):
                     unpack(strip0, strips_dst, (parity,) + melt)
+                    unpack(edge0, edges, (parity,) + melt)
 
         state = (dst, strips_dst, src, strips)
 
@@ -304,18 +306,18 @@
     smem = pl.BlockSpec(memory_space=pltpu.SMEM)
     f32 = jnp.float32
     dma = pltpu.SemaphoreType.DMA
-    main0, strip0 = pl.pallas_call(
+    main0, strip0, edge0 = pl.pallas_call(
         functools.partial(gather_kernel, plan, mesh_shape, levels),
         out_shape=(
             jax.ShapeDtypeStruct((3, plan.tall, plan.deep, width), f32),
             jax.ShapeDtypeStruct((3, 2, plan.deep, width), f32),
+            jax.ShapeDtypeStruct((3, 2, plan.deep, width), f32),
         ),
         in_specs=[vmem, vmem, vmem, smem],
-        out_specs=(vmem, vmem),
+        out_specs=(vmem, vmem, vmem),
         scratch_shapes=[
             pltpu.VMEM((plan.above * rows, width), jnp.int32),
             pltpu.VMEM((2, plan.above * rows, width), f32),
-            pltpu.VMEM((3, 2, plan.deep, width), f32),
             dma((3,)), dma((3,)), dma((12,)), dma((12,)), dma((3,)), dma((3,)),
         ],
         compiler_params=pltpu.CompilerParams(collective_id=0, has_side_effects=True),
@@ -327,16 +329,17 @@
             jax.ShapeDtypeStruct((4, flat, width), f32),
             jax.ShapeDtypeStruct((2, flat, width), f32),
         ),
-        in_specs=[vmem, vmem],
+        in_specs=[vmem, vmem, vmem],
         out_specs=(vmem, vmem),
         scratch_shapes=[
             pltpu.VMEM((6, plan.tall, plan.deep, width), f32),
             pltpu.VMEM((6, plan.tall, plan.deep, width), f32),
             pltpu.VMEM((6, 2, plan.deep, width), f32),
             pltpu.VMEM((6, 2, plan.deep, width), f32),
+            pltpu.VMEM((6, 2, plan.deep, width), f32),
         ],
         name="steps",
-    )(main0, strip0)
+    )(main0, strip0, edge0)
     return phases.reshape(4, planes, rows, width), potentials.reshape(2, planes, rows, width)
 
 

time: 53.3 us -> 40.1 us (0.75)
  Pallas kernels: 52.3 us -> 39.1 us
    pallas_call x1, Pallas kernels: 33.2 us -> 19.9 us  [on_device(): pl.pallas_call(functools.partial(steps_kernel, plan, mesh_shape[0]), out_...]
where the time goes in v2:
time: 40.1 us; the launch traced here: 39.7 us
  Pallas kernels  39.1 us (98%)
  between operations  0.64 us (2%)
    pallas_call x1, Pallas kernels, on_device(): pl.pallas_call(functools.partial(steps_kernel, plan, mesh_shape[0]), out_...  19.9 us
    pallas_call x1, Pallas kernels, on_device(): pl.pallas_call(functools.partial(gather_kernel, plan, mesh_shape, levels)...  19.2 us

profile of v2, /device:TPU:0, one launch (start us, length us, event | category | flops | bytes accessed | tf_op | source)
XLA Modules:
  0.0 39.7 jit_solution(4005230712363232160)
XLA Ops:
  0.6 19.2 %gather.1 = (f32[3,18,48,128]{3,2,1,0:T(8,128)}, f32[3,2,48,128]{3,2,1,0:T(8,128)}, f32[3,2,48,128]{3,2,1,0:T(8,128)}) custom-call(s32[256,128]{1,0:T(8,128)} %bitcast.6, f32[2,256,128]{2,1,0:T(8,128)} %bitcast.5, s32[128,128]{1,0:T(8,128)} %bitcast.7, f32[2,8]{1,0:T(2,128)} %table.1), custom_call_target="tpu_custom_call" | custom-call | tf_op jit(solution)/shard_map/gather/pallas_call | solution.py:309
  19.8 19.9 %steps.1 = (f32[4,256,128]{2,1,0:T(8,128)}, f32[2,256,128]{2,1,0:T(8,128)}) custom-call(f32[3,18,48,128]{3,2,1,0:T(8,128)} %get-tuple-element.7.main0, f32[3,2,48,128]{3,2,1,0:T(8,128)} %get-tuple-element.8.strip0, f32[3,2,48,128]{3,2,1,0:T(8,128)} %get-tuple-element.9.edge0), custom_call_target="tpu_custom_call" | custom-call | tf_op jit(solution)/shard_map/steps/pallas_call | solution.py:326

commit v3 on v2

--- a/solution.py
+++ b/solution.py
@@ -56,100 +56,112 @@
     greet((g, y, z_other))
     pl.semaphore_wait(barrier, 3 + has_below.astype(jnp.int32) + has_above.astype(jnp.int32))
 
-    def g_copy(i):
-        size = plan.above * rows
-        src = lab.at[pl.ds(0, size)] if i == 0 else pot.at[i - 1, pl.ds(0, size)]
-        dst = lab_up if i == 0 else pot_up.at[i - 1]
+    split = (0, plan.upper // 3 // 8 * 8, plan.upper)
+    pieces = [(piece, i) for i in range(3) for piece in range(2)]
+
+    def g_copy(piece, i):
+        begin, end = split[piece], min(split[piece + 1], plan.above)
+        at = pl.ds(begin * rows, (end - begin) * rows)
+        src, dst = (lab.at[at], lab_up.at[at]) if i == 0 else (pot.at[i - 1, at], pot_up.at[i - 1, at])
+        sem = 3 * piece + i
         return pltpu.make_async_remote_copy(
-            src_ref=src, dst_ref=dst, send_sem=g_send.at[i], recv_sem=g_recv.at[i],
+            src_ref=src, dst_ref=dst, send_sem=g_send.at[sem], recv_sem=g_recv.at[sem],
             device_id=(g - 1, y, z), device_id_type=MESH)
 
     @pl.when(has_below)
     def _():
-        for i in range(3):
-            g_copy(i).start()
-
-    def y_copy(slot, values, low, size, up):
-        if up:
-            src, dst, target = rows, 0, y_up
-        else:
-            src, dst, target = STEPS, STEPS + rows, y_down
-        return pltpu.make_async_remote_copy(
-            src_ref=main.at[values, pl.ds(src, STEPS), pl.ds(low, size)],
-            dst_ref=main.at[values, pl.ds(dst, STEPS), pl.ds(low, size)],
-            send_sem=y_send.at[slot], recv_sem=y_recv.at[slot],
-            device_id=(g, target, z), device_id_type=MESH)
+        for piece, i in pieces:
+            g_copy(piece, i).start()
+
+    def y_copies(part, i, low, size):
+        copies = []
+        for up in range(2):
+            src, dst, target = (rows, 0, y_up) if up else (STEPS, STEPS + rows, y_down)
+            sem = 2 * (3 * part + i) + up
+            copy = pltpu.make_async_remote_copy(
+                src_ref=main.at[i, pl.ds(src, STEPS), pl.ds(low, size)],
+                dst_ref=main.at[i, pl.ds(dst, STEPS), pl.ds(low, size)],
+                send_sem=y_send.at[sem], recv_sem=y_recv.at[sem],
+                device_id=(g, target, z), device_id_type=MESH)
+            copy.start()
+            copies.append(copy)
+        return copies
 
     def row_of(ref, i, row, begin, size):
         at = pl.ds(begin * rows + row, size, stride=rows)
         return ref[at].astype(jnp.float32) if i == 0 else ref[i - 1, at]
 
-    own_copies = []
+    y_sent = {}
     for i in range(3):
         for row in range(rows):
             main[i, STEPS + row, 0:own] = row_of(lab if i == 0 else pot, i, row, plan.skip, own)
-        for up in (True, False):
-            copy = y_copy(2 * i + up, i, 0, own, up)
-            copy.start()
-            own_copies.append(copy)
-
-    up_copies = []
-    for i in range(3):
+        y_sent[0, i] = y_copies(0, i, 0, own)
+
+    def z_copy(part, i, low, size):
+        for copy in y_sent[part, i]:
+            copy.wait_recv()
+        lane = lax.broadcasted_iota(jnp.int32, (size, 128), 1)
+        for parity in range(2):
+            packed = jnp.zeros((size, 128), jnp.float32)
+            for slot in range(plan.slots):
+                turned = pltpu.roll(main[i, 2 * slot + parity, low : low + size], WIDE * slot + HALF, 1)
+                packed = jnp.where((lane >= WIDE * slot) & (lane < WIDE * slot + WIDE), turned, packed)
+            pack[i, parity, low : low + size] = packed
+        sem = 3 * part + i
+        at = (i, slice(None), pl.ds(low, size))
+        copy = pltpu.make_async_remote_copy(
+            src_ref=pack.at[at], dst_ref=strip.at[at], send_sem=z_send.at[sem], recv_sem=z_recv.at[sem],
+            device_id=(g, y, z_other), device_id_type=MESH)
+        copy.start()
+        return copy
+
+    def enter(piece, i):
+        begin, end = split[piece], split[piece + 1]
+        filled = min(end, plan.above)
+
         @pl.when(has_above)
-        def _(i=i):
-            g_copy(i).wait_recv()
+        def _():
+            g_copy(piece, i).wait_recv()
             for row in range(rows):
-                main[i, STEPS + row, own : own + plan.above] = row_of(lab_up if i == 0 else pot_up, i, row, 0, plan.above)
-                rest = plan.upper - plan.above
-                if rest:
-                    main[i, STEPS + row, own + plan.above : plan.deep] = jnp.zeros((rest, 128), jnp.float32)
+                main[i, STEPS + row, own + begin : own + filled] = row_of(lab_up if i == 0 else pot_up, i, row, begin, filled - begin)
+                if end > filled:
+                    main[i, STEPS + row, own + filled : own + end] = jnp.zeros((end - filled, 128), jnp.float32)
 
         @pl.when(jnp.logical_not(has_above))
-        def _(i=i):
+        def _():
+            melt_end = min(end, plan.shift)
             for row in range(rows):
                 if i == 0:
-                    main[0, STEPS + row, own : own + plan.shift] = jnp.full((plan.shift, 128), 3.0, jnp.float32)
+                    value = jnp.full((melt_end - begin, 128), 3.0, jnp.float32)
                 else:
-                    code = codes[pl.ds(row, plan.shift, stride=rows)]
-                    value = jnp.zeros((plan.shift, 128), jnp.float32)
+                    code = codes[pl.ds(begin * rows + row, melt_end - begin, stride=rows)]
+                    value = jnp.zeros((melt_end - begin, 128), jnp.float32)
                     for level in range(levels):
                         value = jnp.where(code == level, table[i - 1, level], value)
-                    main[i, STEPS + row, own : own + plan.shift] = value
-                left = plan.deep - own - plan.shift
-                main[i, STEPS + row, own + plan.shift : plan.deep] = jnp.zeros((left, 128), jnp.float32)
-
-        for up in (True, False):
-            copy = y_copy(6 + 2 * i + up, i, own, plan.upper, up)
-            copy.start()
-            up_copies.append(copy)
-
-    lane = lax.broadcasted_iota(jnp.int32, (plan.deep, 128), 1)
-    z_copies = []
+                main[i, STEPS + row, own + begin : own + melt_end] = value
+                if end > melt_end:
+                    main[i, STEPS + row, own + melt_end : own + end] = jnp.zeros((end - melt_end, 128), jnp.float32)
+
+        y_sent[1 + piece, i] = y_copies(1 + piece, i, own + begin, end - begin)
+
+    z_sent = []
     for i in range(3):
-        for copy in own_copies[2 * i : 2 * i + 2] + up_copies[2 * i : 2 * i + 2]:
-            copy.wait_recv()
-        for parity in range(2):
-            packed = jnp.zeros((plan.deep, 128), jnp.float32)
-            for slot in range(plan.slots):
-                turned = pltpu.roll(main[i, 2 * slot + parity], WIDE * slot + HALF, 1)
-                inside = (lane >= WIDE * slot) & (lane < WIDE * slot + WIDE)
-                packed = jnp.where(inside, turned, packed)
-            pack[i, parity] = packed
-        copy = pltpu.make_async_remote_copy(
-            src_ref=pack.at[i], dst_ref=strip.at[i], send_sem=z_send.at[i], recv_sem=z_recv.at[i],
-            device_id=(g, y, z_other), device_id_type=MESH)
-        copy.start()
-        z_copies.append(copy)
-
-    for copy in z_copies:
+        enter(0, i)
+        enter(1, i)
+        z_sent.append(z_copy(0, i, 0, own))
+    for piece, i in pieces:
+        z_sent.append(z_copy(1 + piece, i, own + split[piece], split[piece + 1] - split[piece]))
+
+    for copy in z_sent:
         copy.wait()
-    for copy in own_copies + up_copies:
-        copy.wait_send()
+    for copies in y_sent.values():
+        for copy in copies:
+            copy.wait_send()
 
     @pl.when(has_below)
     def _():
-        for i in range(3):
-            g_copy(i).wait_send()
+        for piece, i in pieces:
+            g_copy(piece, i).wait_send()
 
 
 def cell_step(center, sums):
@@ -209,8 +221,7 @@
 
     moving = (0, 1, 2, 4, 5)
 
-    def main_tile(src, strips, row, low, top, bottom):
-        slot, parity = row // 2, lax.rem(row, 2)
+    def main_tile(src, strips, row, parity, slot, low, top, bottom):
         turn = 128 - (WIDE * slot + HALF)
         center = [src[f, row, pl.ds(low, 8), :] for f in range(6)]
         sums = []
@@ -252,34 +263,39 @@
                     for f in range(6):
                         strips_dst[f, parity, pl.ds(low, 8), :] = new[f]
 
-            def row_step(row, carry):
-                slot, parity = row // 2, lax.rem(row, 2)
-                turn = WIDE * slot + HALF
-                inside = (lane == turn) | (lane == turn - 1)
-                for tile in range(plan.tiles):
-                    low = plan.start + 8 * tile
-                    new = main_tile(src, strips, row, low, top, bottom)
-                    for f in range(6):
-                        dst[f, row, pl.ds(low, 8), :] = new[f]
-                        if f in moving and step < STEPS - 1:
-                            at = (f, parity, pl.ds(low, 8), slice(None))
-                            edges[at] = jnp.where(inside, pltpu.roll(new[f], turn, 1), edges[at])
+            def pair_step(pair, carry):
+                for part in range(2):
+                    row, parity = 2 * pair + step + part, (step + part) % 2
+                    slot = pair + (step + part) // 2
+                    turn = WIDE * slot + HALF
+                    inside = (lane == turn) | (lane == turn - 1)
+                    for tile in range(plan.tiles):
+                        low = plan.start + 8 * tile
+                        new = main_tile(src, strips, row, parity, slot, low, top, bottom)
+                        for f in range(6):
+                            dst[f, row, pl.ds(low, 8), :] = new[f]
+                            if f in moving and step < STEPS - 1:
+                                at = (f, parity, pl.ds(low, 8), slice(None))
+                                edges[at] = jnp.where(inside, pltpu.roll(new[f], turn, 1), edges[at])
                 return carry
 
-            lax.fori_loop(step, tall - step, row_step, 0)
+            lax.fori_loop(0, (tall - 2 * step) // 2, pair_step, 0)
         else:
-            def row_last(row, carry):
-                for tile in range(plan.planes // 8):
-                    low = plan.first + 8 * tile
-                    new = main_tile(src, strips, row + STEPS, low, top, bottom)
-                    at = pl.ds(8 * tile * rows + row, 8, stride=rows)
-                    for f in range(4):
-                        phases[f, at, :] = new[f]
-                    for i in range(2):
-                        potentials[i, at, :] = new[4 + i]
+            def pair_last(pair, carry):
+                for part in range(2):
+                    row, parity = 2 * pair + part, (STEPS + part) % 2
+                    slot = pair + (STEPS + part) // 2
+                    for tile in range(plan.planes // 8):
+                        low = plan.first + 8 * tile
+                        new = main_tile(src, strips, row + STEPS, parity, slot, low, top, bottom)
+                        at = pl.ds(8 * tile * rows + row, 8, stride=rows)
+                        for f in range(4):
+                            phases[f, at, :] = new[f]
+                        for i in range(2):
+                            potentials[i, at, :] = new[4 + i]
                 return carry
 
-            lax.fori_loop(0, rows, row_last, 0)
+            lax.fori_loop(0, rows // 2, pair_last, 0)
         if step == STEPS_BEFORE:
             melt = (slice(plan.own, plan.own + plan.shift), slice(None))
 
@@ -318,7 +334,7 @@
         scratch_shapes=[
             pltpu.VMEM((plan.above * rows, width), jnp.int32),
             pltpu.VMEM((2, plan.above * rows, width), f32),
-            dma((3,)), dma((3,)), dma((12,)), dma((12,)), dma((3,)), dma((3,)),
+            dma((6,)), dma((6,)), dma((18,)), dma((18,)), dma((9,)), dma((9,)),
         ],
         compiler_params=pltpu.CompilerParams(collective_id=0, has_side_effects=True),
         name="gather",

time: 40.1 us -> 34.4 us (0.86)
  Pallas kernels: 39.1 us -> 33.2 us
    pallas_call x1, Pallas kernels: 19.9 us -> 14.6 us  [on_device(): pl.pallas_call(functools.partial(steps_kernel, plan, mesh_shape[0]), out_...]
    pallas_call x1, Pallas kernels: 19.2 us -> 18.6 us  [on_device(): pl.pallas_call(functools.partial(gather_kernel, plan, mesh_shape, levels)...]
where the time goes in v3:
time: 34.4 us; the launch traced here: 33.8 us
  Pallas kernels  33.2 us (97%)
  between operations  0.64 us (2%)
    pallas_call x1, Pallas kernels, on_device(): pl.pallas_call(functools.partial(gather_kernel, plan, mesh_shape, levels)...  18.6 us
    pallas_call x1, Pallas kernels, on_device(): pl.pallas_call(functools.partial(steps_kernel, plan, mesh_shape[0]), out_...  14.6 us

profile of v3, /device:TPU:0, one launch (start us, length us, event | category | flops | bytes accessed | tf_op | source)
XLA Modules:
  0.0 33.8 jit_solution(10783348021148093153)
XLA Ops:
  0.6 18.6 %gather.1 = (f32[3,18,48,128]{3,2,1,0:T(8,128)}, f32[3,2,48,128]{3,2,1,0:T(8,128)}, f32[3,2,48,128]{3,2,1,0:T(8,128)}) custom-call(s32[256,128]{1,0:T(8,128)} %bitcast.6, f32[2,256,128]{2,1,0:T(8,128)} %bitcast.5, s32[128,128]{1,0:T(8,128)} %bitcast.7, f32[2,8]{1,0:T(2,128)} %table.1), custom_call_target="tpu_custom_call" | custom-call | tf_op jit(solution)/shard_map/gather/pallas_call | solution.py:325
  19.2 14.6 %steps.1 = (f32[4,256,128]{2,1,0:T(8,128)}, f32[2,256,128]{2,1,0:T(8,128)}) custom-call(f32[3,18,48,128]{3,2,1,0:T(8,128)} %get-tuple-element.7.main0, f32[3,2,48,128]{3,2,1,0:T(8,128)} %get-tuple-element.8.strip0, f32[3,2,48,128]{3,2,1,0:T(8,128)} %get-tuple-element.9.edge0), custom_call_target="tpu_custom_call" | custom-call | tf_op jit(solution)/shard_map/steps/pallas_call | solution.py:342

commit v4 on v3

--- a/solution.py
+++ b/solution.py
@@ -325,9 +325,9 @@
     main0, strip0, edge0 = pl.pallas_call(
         functools.partial(gather_kernel, plan, mesh_shape, levels),
         out_shape=(
-            jax.ShapeDtypeStruct((3, plan.tall, plan.deep, width), f32),
-            jax.ShapeDtypeStruct((3, 2, plan.deep, width), f32),
-            jax.ShapeDtypeStruct((3, 2, plan.deep, width), f32),
+            pltpu.VMEM((3, plan.tall, plan.deep, width), f32),
+            pltpu.VMEM((3, 2, plan.deep, width), f32),
+            pltpu.VMEM((3, 2, plan.deep, width), f32),
         ),
         in_specs=[vmem, vmem, vmem, smem],
         out_specs=(vmem, vmem, vmem),
@@ -339,6 +339,7 @@
         compiler_params=pltpu.CompilerParams(collective_id=0, has_side_effects=True),
         name="gather",
     )(labels.reshape(flat, width), potential.reshape(2, flat, width), melt_codes.reshape(shift * rows, width), melt_table)
+    main0, strip0, edge0 = (pltpu.with_memory_space_constraint(v, pltpu.VMEM) for v in (main0, strip0, edge0))
     phases, potentials = pl.pallas_call(
         functools.partial(steps_kernel, plan, mesh_shape[0]),
         out_shape=(

time: 34.4 us -> 31.8 us (0.924)
  Pallas kernels: 33.2 us -> 30.6 us
    pallas_call x1, Pallas kernels: 14.6 us -> 13.2 us  [on_device(): pl.pallas_call(functools.partial(steps_kernel, plan, mesh_shape[0]), out_...]
    pallas_call x1, Pallas kernels: 18.6 us -> 17.4 us  [on_device(): pl.pallas_call(functools.partial(gather_kernel, plan, mesh_shape, levels)...]
where the time goes in v4:
time: 31.8 us; the launch traced here: 31.3 us
  Pallas kernels  30.6 us (96%)
  between operations  0.64 us (2%)
    pallas_call x1, Pallas kernels, on_device(): pl.pallas_call(functools.partial(gather_kernel, plan, mesh_shape, levels)...  17.4 us
    pallas_call x1, Pallas kernels, on_device(): pl.pallas_call(functools.partial(steps_kernel, plan, mesh_shape[0]), out_...  13.2 us

profile of v4, /device:TPU:0, one launch (start us, length us, event | category | flops | bytes accessed | tf_op | source)
XLA Modules:
  0.0 31.3 jit_solution(4246636901415235947)
XLA Ops:
  0.6 17.4 %gather.1 = (f32[3,18,48,128]{3,2,1,0:T(8,128)S(1)}, f32[3,2,48,128]{3,2,1,0:T(8,128)S(1)}, f32[3,2,48,128]{3,2,1,0:T(8,128)S(1)}) custom-call(s32[256,128]{1,0:T(8,128)} %bitcast.6, f32[2,256,128]{2,1,0:T(8,128)} %bitcast.5, s32[128,128]{1,0:T(8,128)} %bitcast.7, f32[2,8]{1,0:T(2,128)} %table.1), custom_call_target="tpu_custom_call" | custom-call | tf_op jit(solution)/shard_map/gather/pallas_call | solution.py:325
  18.1 13.2 %steps.1 = (f32[4,256,128]{2,1,0:T(8,128)}, f32[2,256,128]{2,1,0:T(8,128)}) custom-call(f32[3,18,48,128]{3,2,1,0:T(8,128)S(1)} %get-tuple-element.7.main0, f32[3,2,48,128]{3,2,1,0:T(8,128)S(1)} %get-tuple-element.8.strip0, f32[3,2,48,128]{3,2,1,0:T(8,128)S(1)} %get-tuple-element.9.edge0), custom_call_target="tpu_custom_call" | custom-call | tf_op jit(solution)/shard_map/steps/pallas_call | solution.py:343

commit v5 on v4

--- a/solution.py
+++ b/solution.py
@@ -263,10 +263,13 @@
                     for f in range(6):
                         strips_dst[f, parity, pl.ds(low, 8), :] = new[f]
 
-            def pair_step(pair, carry):
-                for part in range(2):
-                    row, parity = 2 * pair + step + part, (step + part) % 2
-                    slot = pair + (step + part) // 2
+            count = tall - 2 * step
+            group = 4 if count % 4 == 0 else 2
+
+            def pair_step(pair, carry, step=step, group=group):
+                for part in range(group):
+                    row, parity = group * pair + step + part, (step + part) % 2
+                    slot = group // 2 * pair + (step + part) // 2
                     turn = WIDE * slot + HALF
                     inside = (lane == turn) | (lane == turn - 1)
                     for tile in range(plan.tiles):
@@ -279,7 +282,7 @@
                                 edges[at] = jnp.where(inside, pltpu.roll(new[f], turn, 1), edges[at])
                 return carry
 
-            lax.fori_loop(0, (tall - 2 * step) // 2, pair_step, 0)
+            lax.fori_loop(0, count // group, pair_step, 0)
         else:
             def pair_last(pair, carry):
                 for part in range(2):

time: 31.8 us -> 53 us (1.67)
  Pallas kernels: 30.6 us -> 51.9 us
    pallas_call x1, Pallas kernels: 13.2 us -> 34.4 us  [on_device(): pl.pallas_call(functools.partial(steps_kernel, plan, mesh_shape[0]), out_...]
where the time goes in v5:
time: 53 us; the launch traced here: 52.5 us
  Pallas kernels  51.9 us (98%)
  between operations  0.64 us (1%)
    pallas_call x1, Pallas kernels, on_device(): pl.pallas_call(functools.partial(steps_kernel, plan, mesh_shape[0]), out_...  34.4 us
    pallas_call x1, Pallas kernels, on_device(): pl.pallas_call(functools.partial(gather_kernel, plan, mesh_shape, levels)...  17.4 us

profile of v5, /device:TPU:0, one launch (start us, length us, event | category | flops | bytes accessed | tf_op | source)
XLA Modules:
  0.0 52.5 jit_solution(2759056981660736103)
XLA Ops:
  0.6 17.4 %gather.1 = (f32[3,18,48,128]{3,2,1,0:T(8,128)S(1)}, f32[3,2,48,128]{3,2,1,0:T(8,128)S(1)}, f32[3,2,48,128]{3,2,1,0:T(8,128)S(1)}) custom-call(s32[256,128]{1,0:T(8,128)} %bitcast.6, f32[2,256,128]{2,1,0:T(8,128)} %bitcast.5, s32[128,128]{1,0:T(8,128)} %bitcast.7, f32[2,8]{1,0:T(2,128)} %table.1), custom_call_target="tpu_custom_call" | custom-call | tf_op jit(solution)/shard_map/gather/pallas_call | solution.py:328
  18.1 34.4 %steps.1 = (f32[4,256,128]{2,1,0:T(8,128)}, f32[2,256,128]{2,1,0:T(8,128)}) custom-call(f32[3,18,48,128]{3,2,1,0:T(8,128)S(1)} %get-tuple-element.7.main0, f32[3,2,48,128]{3,2,1,0:T(8,128)S(1)} %get-tuple-element.8.strip0, f32[3,2,48,128]{3,2,1,0:T(8,128)S(1)} %get-tuple-element.9.edge0), custom_call_target="tpu_custom_call" | custom-call | tf_op jit(solution)/shard_map/steps/pallas_call | solution.py:346
